TPU v7x, 128 devices: a whole 4x4x4 slice. The times are simulated.
128 devices in a mesh: dp: 32 (over z, x, y_lo), tensor: 4 (over y_hi, core).
Axes of the slice: x: 4, y: 4 (y_hi: 2, y_lo: 2; y = y_hi * 2 + y_lo), z: 4, core: 2. Of those that a mesh axis runs over, the one named last changes fastest.
Arguments:
- acts: bfloat16 [16384, 4096], P(('dp', 'tensor')), may hold values from -6 to 6
- out_grad: bfloat16 [16384, 16384], P('dp', 'tensor'), may hold values from -0.09375 to 0.09375
- projector: bfloat16 [4096, 512], replicated, may hold values from -0.09375 to 0.09375
- weight: bfloat16 [4096, 16384], P('dp', 'tensor'), may hold values from -6 to 6
- first_moment: float32 [4, 4096, 512], P('tensor', 'dp'), may hold values from -4 to 4
- second_moment: float32 [4, 4096, 512], P('tensor', 'dp'), may hold values from 0.01 to 1
Outputs:
- new_weight: bfloat16 [4096, 16384], P('dp', 'tensor')
- new_first: float32 [4, 4096, 512], P('tensor', 'dp')
- new_second: float32 [4, 4096, 512], P('tensor', 'dp')
All inputs are finite; a program needn't handle non-finite values.
Results may differ from a plain program's by a relative error of at most 0.015.
Values may be sent and summed in bfloat16 or wider, within the bound.
A program may use at most 128 MiB of HBM per device.

v0:
```python
import jax
import jax.numpy as jnp
from jax import lax
from jax.sharding import PartitionSpec as P

beta_first = 0.9
beta_second = 0.95
adam_step = 10
epsilon = 1e-08
step_rate = 0.5


def adam_moments(lowgrad, first_moment, second_moment):
    new_first = beta_first * first_moment + (1.0 - beta_first) * lowgrad
    new_second = beta_second * second_moment + (1.0 - beta_second) * lowgrad * lowgrad
    corrected_first = new_first / (1.0 - beta_first**adam_step)
    corrected_second = new_second / (1.0 - beta_second**adam_step)
    direction = (corrected_first / (jnp.sqrt(corrected_second) + epsilon)).astype(jnp.bfloat16)
    return (new_first, new_second, direction)


def per_device(acts, out_grad, projector, weight, first_moment, second_moment):
    whole_acts = lax.all_gather(acts, "tensor", axis=0, tiled=True)
    owned_grad = lax.psum_scatter(
        lax.dot_general(
            out_grad, whole_acts, (((0,), (0,)), ((), ())), preferred_element_type=jnp.float32
        ).astype(jnp.bfloat16),
        "dp",
        scatter_dimension=0,
        tiled=True,
    ).astype(jnp.float32)
    lowgrad = jnp.dot(
        owned_grad,
        projector.astype(jnp.float32),
        precision=lax.Precision.HIGHEST,
        preferred_element_type=jnp.float32,
    )
    new_first, new_second, direction = adam_moments(lowgrad, first_moment[0], second_moment[0])
    owned_update = lax.dot_general(
        projector, direction, (((1,), (1,)), ((), ())), preferred_element_type=jnp.float32
    ).astype(jnp.bfloat16)
    update = lax.all_to_all(owned_update, "dp", split_axis=0, concat_axis=1, tiled=True)
    new_weight = (weight.astype(jnp.float32) - step_rate * update.astype(jnp.float32)).astype(
        jnp.bfloat16
    )
    return (new_weight, new_first[None], new_second[None])


def solution(mesh):
    return jax.shard_map(
        per_device,
        mesh=mesh,
        in_specs=(
            P(("dp", "tensor"), None),
            P("dp", "tensor"),
            P(),
            P("dp", "tensor"),
            P("tensor", "dp", None),
            P("tensor", "dp", None),
        ),
        out_specs=(P("dp", "tensor"), P("tensor", "dp", None), P("tensor", "dp", None)),
        check_vma=False,
    )
```

profile of v0, /device:TPU:0, one launch (start us, length us, event | category | flops | bytes accessed | tf_op | source)
XLA Modules:
  0.0 826.6 jit_solution(7803383295628024617)
XLA Ops:
  7.2 0.0 all-gather.2.cloned.1.call-start
  7.2 0.7 all-gather.2.cloned.1.call-update
  7.9 0.0 reduce-scatter.2.cloned.1.call-start
  7.9 42.8 %all-gather.2.cloned.1.call-done = bf16[512,4096]{1,0:T(8,128)(2,1)} async-done(((bf16[128,4096]{1,0:T(8,128)(2,1)}), bf16[512,4096]{1,0:T(8,128)(2,1)}) %all-gather.2.cloned.1.call-update) | async-done | bytes 4194320 | tf_op jit(solution)/shard_map/all_gather | solution.py:23
  50.7 24.1 %convolution_convert_fusion = bf16[4096,4096]{1,0:T(8,128)(2,1)} fusion(bf16[512,4096]{1,0:T(8,128)(2,1)} %param.7, bf16[512,4096]{1,0:T(8,128)(2,1)} %all-gather.2.cloned.1.call-done), kind=kOutput, calls=%fused_computation | convolution fusion | flops 17196646400 | bytes 41943040 | tf_op jit(solution)/shard_map/dot_general | solution.py:25
  74.8 0.0 reduce-scatter.2.cloned.1.call-update
  74.9 0.0 copy-start.1
  74.9 0.0 copy-start.2
  74.9 708.0 %reduce-scatter.2.cloned.1.call-done = bf16[128,4096]{1,0:T(8,128)(2,1)} async-done(((bf16[4096,4096]{1,0:T(8,128)(2,1)}), bf16[128,4096]{1,0:T(8,128)(2,1)}) %reduce-scatter.2.cloned.1.call-update) | async-done | bytes 1048592 | tf_op jit(solution)/shard_map/reduce_scatter | solution.py:24
  782.9 0.0 copy-start
  782.9 3.4 fusion.15
  786.2 0.0 copy-done.1
  786.3 0.0 copy-done.2
  786.3 0.3 copy-done
  786.6 1.4 fusion
  788.1 1.3 copy.14
  789.3 7.3 all-to-all-start
  796.6 0.9 fusion.6
  797.5 17.2 %all-to-all-done = bf16[32,128,128]{1,2,0:T(8,128)(2,1)S(1)} async-done(((bf16[32,128,128]{1,2,0:T(8,128)(2,1)}), bf16[32,128,128]{1,2,0:T(8,128)(2,1)S(1)}, u32[]{:S(2)}, u32[]{:S(2)}) %all-to-all-start) | async-done | bytes 1048608 | tf_op jit(solution)/shard_map/all_to_all | solution.py:42
  814.7 0.2 convert_multiply_fusion
  814.9 1.9 copy.11
  816.8 3.0 subtract_convert_fusion
Async XLA Ops:
  7.2 43.5 %all-gather.2.cloned.1.call-start = ((), (), s32[]{:S(2)}) async-start(), calls=%async_computation.2 | async-start | bytes 5242880 | tf_op jit(solution)/shard_map/all_gather | solution.py:23
  7.9 775.0 %reduce-scatter.2.cloned.1.call-start = ((), (), s32[]{:S(2)}) async-start(), calls=%async_computation.3 | async-start | bytes 34603008 | tf_op jit(solution)/shard_map/reduce_scatter | solution.py:24
  74.9 711.4 %copy-start.1 = (f32[1,128,512]{2,1,0:T(8,128)S(1)}, f32[1,128,512]{2,1,0:T(8,128)}, u32[]{:S(2)}) copy-start(f32[1,128,512]{2,1,0:T(8,128)} %param.10) | copy-start | bytes 786436
  74.9 711.4 %copy-start.2 = (f32[1,128,512]{2,1,0:T(8,128)S(1)}, f32[1,128,512]{2,1,0:T(8,128)}, u32[]{:S(2)}) copy-start(f32[1,128,512]{2,1,0:T(8,128)} %param.11) | copy-start | bytes 786436
  782.9 3.7 copy-start
  789.3 25.3 %all-to-all-start = ((bf16[32,128,128]{1,2,0:T(8,128)(2,1)}), bf16[32,128,128]{1,2,0:T(8,128)(2,1)S(1)}, u32[]{:S(2)}, u32[]{:S(2)}) async-start(bf16[32,128,128]{1,2,0:T(8,128)(2,1)} %bitcast.31), calls=%async_computation.1 | async-start | bytes 2097152 | tf_op jit(solution)/shard_map/all_to_all | solution.py:42
Sparse Core Ops, SparseCore 0:
  9.7 40.9 all-gather.1
  75.0 707.8 reduce-scatter.1
where the time goes:
time: 827 us
  waiting for transfers between devices  769 us (93%)
  matrix products  29 us (4%)
  between operations  14.1 us (2%)
    reduce_scatter x1, waiting for transfers between devices, per_device(): lax.psum_scatter(lax.dot_general(out_grad, whole_acts, (((0,), (0,)), (()...  708 us
    all_gather x1, waiting for transfers between devices, per_device(): whole_acts = lax.all_gather(acts, 'tensor', axis=0, tiled=True)  42.8 us
    dot_general x1, matrix products, per_device(): lax.dot_general(out_grad, whole_acts, (((0,), (0,)), ((), ())), preferred...  24.1 us
    all_to_all x1, waiting for transfers between devices, per_device(): lax.all_to_all(owned_update, 'dp', split_axis=0, concat_axis=1, tiled=True)  17.2 us
  transfers between devices with their start and end apart: 3, of which 3 were waited for; matrix products, arithmetic and copies ran while one was open for 0% of the time, Pallas kernels for 0%

commit v1 on v0

--- a/solution.py
+++ b/solution.py
@@ -20,7 +20,9 @@
 
 
 def per_device(acts, out_grad, projector, weight, first_moment, second_moment):
-    whole_acts = lax.all_gather(acts, "tensor", axis=0, tiled=True)
+    whole_acts = jnp.concatenate(
+        lax.all_to_all(jnp.stack([acts] * lax.axis_size("tensor")), "tensor", 0, 0), axis=0
+    )
     owned_grad = lax.psum_scatter(
         lax.dot_general(
             out_grad, whole_acts, (((0,), (0,)), ((), ())), preferred_element_type=jnp.float32

time: 827 us -> 837 us (1.012)
  blocking collectives: 0 us -> 54.3 us
  waiting for transfers between devices: 769 us -> 726 us
    all_to_all x0 -> x1, blocking collectives: none -> 54.3 us  [per_device(): lax.all_to_all(jnp.stack([acts] * lax.axis_size('tensor')), 'tensor', 0, 0)]
    all_gather x1 -> x0, waiting for transfers between devices: 42.8 us -> none  [per_device(): whole_acts = lax.all_gather(acts, 'tensor', axis=0, tiled=True)]
  transfers between devices with their start and end apart: 3 -> 2, of which waited for: 3 -> 2; matrix products, arithmetic and copies ran while one was open for 0% -> 0% of each run, Pallas kernels for 0% -> 0%
where the time goes in v1:
time: 837 us
  waiting for transfers between devices  726 us (87%)
  blocking collectives  54.3 us (6%)
  matrix products  26.4 us (3%)
  between operations  14.1 us (2%)
    reduce_scatter x1, waiting for transfers between devices, per_device(): lax.psum_scatter(lax.dot_general(out_grad, whole_acts, (((0,), (0,)), (()...  708 us
    all_to_all x1, blocking collectives, per_device(): lax.all_to_all(jnp.stack([acts] * lax.axis_size('tensor')), 'tensor', 0, 0)  54.3 us
    dot_general x1, matrix products, per_device(): lax.dot_general(out_grad, whole_acts, (((0,), (0,)), ((), ())), preferred...  21.6 us
    all_to_all x1, waiting for transfers between devices, per_device(): lax.all_to_all(owned_update, 'dp', split_axis=0, concat_axis=1, tiled=True)  17.2 us
  transfers between devices with their start and end apart: 2, of which 2 were waited for; matrix products, arithmetic and copies ran while one was open for 0% of the time, Pallas kernels for 0%

profile of v1, /device:TPU:0, one launch (start us, length us, event | category | flops | bytes accessed | tf_op | source)
XLA Modules:
  0.0 837.2 jit_solution(7284702812043701777)
XLA Ops:
  7.2 0.0 reduce-scatter.2.cloned.1.call-start
  7.2 1.7 stack.2
  8.9 0.0 copy-start.3
  8.9 54.3 %all_to_all.18 = bf16[4,128,4096]{2,1,0:T(8,128)(2,1)S(1)} all-to-all(bf16[4,128,4096]{2,1,0:T(8,128)(2,1)S(1)} %stack.2), channel_id=1, replica_groups=mesh['dp'=32,'tensor'=4] {'tensor'}, dimensions={0} | all-to-all | bytes 8388608 | tf_op jit(solution)/shard_map/all_to_all | solution.py:24
  63.2 0.0 copy-done.3
  63.2 21.6 %convolution_convert_fusion = bf16[4096,4096]{1,0:T(8,128)(2,1)} fusion(bf16[512,4096]{1,0:T(8,128)(2,1)S(1)} %copy-done.3, bf16[512,4096]{1,0:T(8,128)(2,1)S(1)} %bitcast.34), kind=kOutput, calls=%fused_computation | convolution fusion | flops 17196646400 | bytes 41943040 | tf_op jit(solution)/shard_map/dot_general | solution.py:27
  84.9 0.0 reduce-scatter.2.cloned.1.call-update
  84.9 0.0 copy-start.1
  84.9 0.0 copy-start.2
  84.9 708.5 %reduce-scatter.2.cloned.1.call-done = bf16[128,4096]{1,0:T(8,128)(2,1)} async-done(((bf16[4096,4096]{1,0:T(8,128)(2,1)}), bf16[128,4096]{1,0:T(8,128)(2,1)}) %reduce-scatter.2.cloned.1.call-update) | async-done | bytes 1048592 | tf_op jit(solution)/shard_map/reduce_scatter | solution.py:26
  793.4 0.0 copy-start
  793.4 3.4 fusion.15
  796.7 0.0 copy-done.1
  796.8 0.0 copy-done.2
  796.8 0.3 copy-done
  797.1 1.4 fusion
  798.6 1.3 copy.14
  799.8 7.3 all-to-all-start.1
  807.1 0.9 fusion.6
  808.0 17.2 %all-to-all-done.1 = bf16[32,128,128]{1,2,0:T(8,128)(2,1)S(1)} async-done(((bf16[32,128,128]{1,2,0:T(8,128)(2,1)}), bf16[32,128,128]{1,2,0:T(8,128)(2,1)S(1)}, u32[]{:S(2)}, u32[]{:S(2)}) %all-to-all-start.1) | async-done | bytes 1048608 | tf_op jit(solution)/shard_map/all_to_all | solution.py:44
  825.2 0.2 convert_multiply_fusion
  825.4 1.9 copy.11
  827.3 3.0 subtract_convert_fusion
Async XLA Ops:
  7.2 786.2 %reduce-scatter.2.cloned.1.call-start = ((), (), s32[]{:S(2)}) async-start(), calls=%async_computation.3 | async-start | bytes 34603008 | tf_op jit(solution)/shard_map/reduce_scatter | solution.py:26
  8.9 54.3 %copy-start.3 = (bf16[512,4096]{1,0:T(8,128)(2,1)S(1)}, bf16[512,4096]{1,0:T(8,128)(2,1)}, u32[]{:S(2)}) copy-start(bf16[512,4096]{1,0:T(8,128)(2,1)} %param.7) | copy-start | bytes 12582916
  84.9 711.9 %copy-start.1 = (f32[1,128,512]{2,1,0:T(8,128)S(1)}, f32[1,128,512]{2,1,0:T(8,128)}, u32[]{:S(2)}) copy-start(f32[1,128,512]{2,1,0:T(8,128)} %param.10) | copy-start | bytes 786436
  84.9 711.9 %copy-start.2 = (f32[1,128,512]{2,1,0:T(8,128)S(1)}, f32[1,128,512]{2,1,0:T(8,128)}, u32[]{:S(2)}) copy-start(f32[1,128,512]{2,1,0:T(8,128)} %param.11) | copy-start | bytes 786436
  793.4 3.7 copy-start
  799.8 25.4 %all-to-all-start.1 = ((bf16[32,128,128]{1,2,0:T(8,128)(2,1)}), bf16[32,128,128]{1,2,0:T(8,128)(2,1)S(1)}, u32[]{:S(2)}, u32[]{:S(2)}) async-start(bf16[32,128,128]{1,2,0:T(8,128)(2,1)} %bitcast.32), calls=%async_computation.2 | async-start | bytes 2097152 | tf_op jit(solution)/shard_map/all_to_all | solution.py:44
Sparse Core Ops, SparseCore 0:
  85.0 708.3 reduce-scatter.1
